TPU v7x, 128 devices: a whole 4x4x4 slice. The times are simulated.
128 devices in a mesh: gy: 16 (over z_hi, x, core), gz: 8 (over z_lo, y).
Axes of the slice: x: 4, y: 4, z: 4 (z_hi: 2, z_lo: 2; z = z_hi * 2 + z_lo), core: 2. Of those that a mesh axis runs over, the one named last changes fastest.
Arguments:
- reference_image: bfloat16 [64, 1024, 4096], P(None, 'gy', 'gz'), may hold values from -6 to 6
- deformed: bfloat16 [64, 1024, 4096], P(None, 'gy', 'gz'), may hold values from -12 to 12
- displacement: bfloat16 [3, 64, 1024, 4096], P(None, None, 'gy', 'gz'), may hold values from -1 to 1
- plane_factors: float32 [2, 32, 8, 128], P(None, None, None, 'gy'), may hold values from -2.5 to 2.5
- depth_factors: float32 [2, 32, 4096], P(None, None, 'gz'), may hold values from -6 to 6
Outputs:
- residual: bfloat16 [64, 1024, 4096], P(None, 'gy', 'gz')
- step_plane: float32 [2, 32, 8, 128], P(None, None, None, 'gy')
- step_depth: float32 [2, 32, 4096], P(None, None, 'gz')
All inputs are finite; a program needn't handle non-finite values.
Results may differ from a plain program's by a relative error of at most 0.0004.
Values may be sent and summed in bfloat16 or wider, within the bound.
A program may use at most 256 MiB of HBM per device.

v0:
```python
import jax
import jax.numpy as jnp
from jax import lax
from jax.sharding import PartitionSpec as P

RANK = 32
KNOT = 8
epsilon = 1e-06
damping = 0.01
highest = lax.Precision.HIGHEST


def extended(cells, sides, width):
    for axis, dim in sides:
        count = lax.axis_size(axis)
        ends = count - 1
        head = lax.slice_in_dim(cells, 0, width, axis=dim)
        tail = lax.slice_in_dim(cells, cells.shape[dim] - width, cells.shape[dim], axis=dim)
        cells = jnp.concatenate(
            [
                lax.ppermute(tail, axis, [(i, (i + 1) % count) for i in range(ends)]),
                cells,
                lax.ppermute(head, axis, [((i + 1) % count, i) for i in range(ends)]),
            ],
            axis=dim,
        )
    return cells


def tent_weights(shift):
    moved = shift.astype(jnp.float32)
    return [jnp.maximum(0.0, 1.0 - jnp.abs(moved - offset)) for offset in (-1.0, 0.0, 1.0)]


def warp_image(padded, displacement):
    depth_x, width_y, width_z = displacement.shape[1:]
    weight_x = tent_weights(displacement[0])
    weight_y = tent_weights(displacement[1])
    weight_z = tent_weights(displacement[2])
    summed = jnp.zeros((depth_x, width_y, width_z), jnp.float32)
    for along_x in range(3):
        for along_y in range(3):
            partial_z = jnp.zeros((depth_x, width_y, width_z), jnp.float32)
            for along_z in range(3):
                window = padded[
                    along_x : along_x + depth_x,
                    along_y : along_y + width_y,
                    along_z : along_z + width_z,
                ]
                partial_z = partial_z + weight_z[along_z] * window.astype(jnp.float32)
            summed = summed + weight_x[along_x] * weight_y[along_y] * partial_z
    return summed


def expand_nodes(nodes):
    return jnp.repeat(jnp.repeat(nodes, KNOT, axis=2), KNOT, axis=3)


def reduce_nodes(field):
    leading = field.shape[:-2]
    depth_x, width_y = field.shape[-2:]
    shaped = field.reshape(leading + (depth_x // KNOT, KNOT, width_y // KNOT, KNOT))
    return jnp.sum(shaped, axis=(-3, -1))


def contract_rank(left, right):
    return lax.dot_general(left, right, (((0,), (0,)), ((), ())), precision=highest)


def contract_cells(left, right):
    return jnp.dot(left, right, precision=highest)


def contract_depth(left, right):
    return lax.dot_general(left, right, (((1,), (1,)), ((), ())), precision=highest)


def strip_terms(image, padded, displacement, plane_voxels, depth_factors):
    depth_x, width_y, width_z = image.shape
    cells = depth_x * width_y
    warped = warp_image(padded, displacement).reshape(cells, width_z)
    values = image.astype(jnp.float32).reshape(cells, width_z)
    flat_plane = plane_voxels.reshape(2, plane_voxels.shape[1], cells)
    contrast = contract_rank(flat_plane[0], depth_factors[0])
    brightness = contract_rank(flat_plane[1], depth_factors[1])
    misfit = warped - contrast * values - brightness
    product = misfit * values
    squares = values * values
    grad_depth = -jnp.stack(
        [contract_cells(flat_plane[0], product), contract_cells(flat_plane[1], misfit)]
    )
    level_sum = jnp.sum(flat_plane[1] * flat_plane[1], axis=1)
    first_depth = contract_cells(flat_plane[0] * flat_plane[0], squares)
    grad_voxels = -jnp.stack(
        [contract_depth(depth_factors[0], product), contract_depth(depth_factors[1], misfit)]
    )
    diag_voxels = contract_depth(depth_factors[0] * depth_factors[0], squares)
    grad_plane = reduce_nodes(grad_voxels.reshape(2, -1, depth_x, width_y))
    first_diag = reduce_nodes(diag_voxels.reshape(-1, depth_x, width_y))
    depth_level = KNOT * KNOT * jnp.sum(depth_factors[1] * depth_factors[1], axis=1)
    squared_sum = jnp.sum(misfit * misfit)
    residual = misfit.reshape(depth_x, width_y, width_z).astype(jnp.bfloat16)
    return (
        residual,
        squared_sum,
        grad_plane,
        first_diag,
        depth_level,
        grad_depth,
        first_depth,
        level_sum,
    )


def local(reference_image, deformed, displacement, plane_factors, depth_factors):
    rimmed = extended(deformed, (("gy", 1), ("gz", 2)), 1)
    padded = jnp.pad(rimmed, ((1, 1), (0, 0), (0, 0)))
    plane_voxels = expand_nodes(plane_factors)
    (
        residual,
        local_energy,
        grad_plane,
        first_diag,
        depth_level,
        grad_depth,
        first_depth,
        level_sum,
    ) = strip_terms(reference_image, padded, displacement, plane_voxels, depth_factors)
    nodes_x = plane_factors.shape[2]
    nodes_y = plane_factors.shape[3] * lax.axis_size("gy")
    full_z = depth_factors.shape[2] * lax.axis_size("gz")
    energy = lax.psum(local_energy, ("gy", "gz"))
    grad_plane, first_diag, depth_level = lax.psum((grad_plane, first_diag, depth_level), "gz")
    diag_plane = jnp.stack(
        [first_diag, jnp.broadcast_to(depth_level[:, None, None], first_diag.shape)]
    )
    lam_plane = damping * RANK * energy / (nodes_x * nodes_y)
    lam_depth = damping * energy / full_z
    step_plane = -grad_plane / (diag_plane + lam_plane + epsilon)
    grad_depth, first_depth, level_sum = lax.psum((grad_depth, first_depth, level_sum), "gy")
    diag_depth = jnp.stack([first_depth, jnp.broadcast_to(level_sum[:, None], first_depth.shape)])
    step_depth = -grad_depth / (diag_depth + lam_depth + epsilon)
    return (residual, step_plane, step_depth)


def solution(mesh):
    placed = (
        P(None, "gy", "gz"),
        P(None, "gy", "gz"),
        P(None, None, "gy", "gz"),
        P(None, None, None, "gy"),
        P(None, None, "gz"),
    )
    return jax.shard_map(
        local,
        mesh=mesh,
        in_specs=placed,
        out_specs=(P(None, "gy", "gz"), P(None, None, None, "gy"), P(None, None, "gz")),
        check_vma=False,
    )
```

profile of v0, /device:TPU:7, one launch (start us, length us, event | category | flops | bytes accessed | tf_op | source)
XLA Modules:
  0.0 613.2 jit_solution(7184010167852653225)
XLA Ops:
  7.2 0.0 all-reduce.5.cloned.1.call-start
  7.2 1.4 fusion.133
  8.7 6.0 collective-permute-start
  14.7 0.0 copy-start.4
  14.7 2.2 collective-permute-start.1
  16.9 9.0 %fusion.132 = (bf16[1,64,64,512]{3,2,1,0:T(8,128)(2,1)}, bf16[1,64,64,512]{3,2,1,0:T(8,128)(2,1)}, bf16[1,64,64,512]{3,2,1,0:T(8,128)(2,1)}) fusion(bf16[3,64,64,512]{3,2,1,0:T(8,128)(2,1)} %param.7), kind=kLoop, calls=%fused_computation.173 | loop fusion | bytes 25165824 | tf_op jit(solution)/shard_map/slice | solution.py:39
  25.9 0.1 fusion.122
  26.1 0.3 broadcast_in_dim.28
  26.4 8.8 %fusion.124 = f32[4096,512]{1,0:T(8,128)} fusion(f32[32,4096]{0,1:T(8,128)S(1)} %bitcast.293, f32[2,32,512]{2,1,0:T(8,128)S(1)} %copy-done.5), kind=kOutput, calls=%fused_computation.159 | convolution fusion | flops 805306368 | bytes 10551296 | tf_op jit(solution)/shard_map/dot_general | solution.py:67
  35.2 1.2 convert_multiply_fusion
  36.5 7.4 %convolution_reduce_fusion = f32[32,8,8]{0,2,1:T(8,128)} fusion(f32[8,8,8,8,512]{4,3,2,1,0:T(8,128)S(1)} %bitcast.291, f32[2,32,512]{2,1,0:T(8,128)S(1)} %copy-done.5), kind=kOutput, calls=%fused_computation.139 | convolution fusion | flops 805451776 | bytes 8462336 | tf_op jit(solution)/shard_map/dot_general | solution.py:75
  43.9 0.3 broadcast_in_dim.34
  44.2 5.7 convolution_bitcast_fusion.2
  49.8 0.5 broadcast_multiply_fusion
  50.4 13.0 %copy.49 = bf16[64,64,512]{1,0,2:T(8,128)(2,1)} copy(bf16[64,64,512]{2,1,0:T(8,128)(2,1)} %param.6) | data formatting | bytes 8388608 | tf_op args[1]
  63.4 0.2 copy.59
  63.5 12.7 %copy.48 = bf16[64,1,512]{1,0,2:T(8,128)(2,1)} copy(bf16[64,1,512]{2,0,1:T(8,128)(2,1)S(1)} %collective-permute-done) | data formatting | bytes 131072 | tf_op jit(solution)/shard_map/ppermute | solution.py:21
  76.2 12.7 %copy.50 = bf16[64,1,512]{1,0,2:T(8,128)(2,1)} copy(bf16[64,1,512]{2,0,1:T(8,128)(2,1)S(1)} %collective-permute-done.1) | data formatting | bytes 131072 | tf_op jit(solution)/shard_map/ppermute | solution.py:23
  88.9 0.9 pad_maximum_fusion.5
  89.8 3.2 collective-permute-start.2
  93.0 1.3 collective-permute-start.3
  94.3 0.3 broadcast_reduce_fusion
  94.6 13.4 %copy.61 = bf16[1,64,64,512]{2,1,3,0:T(8,128)(2,1)} copy(bf16[1,64,64,512]{3,2,1,0:T(8,128)(2,1)} %get-tuple-element.14) | data formatting | bytes 8388608
  108.0 13.0 %copy.62 = bf16[1,64,64,512]{2,1,3,0:T(8,128)(2,1)} copy(bf16[1,64,64,512]{3,2,1,0:T(8,128)(2,1)} %get-tuple-element.13) | data formatting | bytes 8388608
  121.0 12.9 %copy.63 = bf16[1,64,64,512]{2,1,3,0:T(8,128)(2,1)} copy(bf16[1,64,64,512]{3,2,1,0:T(8,128)(2,1)} %get-tuple-element.12) | data formatting | bytes 8388608
  133.9 32.9 %psum.55 = f32[32]{0:T(128)S(1)} all-reduce(f32[32]{0:T(128)S(1)} %broadcast_reduce_fusion), channel_id=1, replica_groups=mesh['gy'=16,'gz'=8] {'gy'}, use_global_device_ids=true, to_apply=%region_11.12 | all-reduce | flops 32 | bytes 256 | tf_op jit(solution)/shard_map/psum | solution.py:140
  166.8 24.1 %maximum_maximum_fusion = (bf16[64,66,513]{1,0,2:T(8,128)(2,1)S(1)}, bf16[64,66,513]{1,0,2:T(8,128)(2,1)}) fusion(bf16[64,1,512]{1,0,2:T(8,128)(2,1)} %copy.50, bf16[64,64,512]{1,0,2:T(8,128)(2,1)} %copy.49, bf16[64,1,512]{1,0,2:T(8,128)(2,1)} %copy.48, bf16[64,66,1]{1,0,2:T(8,128)(2,1)S(1)} %collective-permute-done.2, ...), kind=kLoop, calls=%fused_computation.126 | loop fusion | flops 34670592 | bytes 13009920 | tf_op jit(solution)/shard_map/concatenate | solution.py:19
  190.8 24.0 %select_maximum_fusion = bf16[66,66,514]{1,0,2:T(8,128)(2,1)S(1)} fusion(bf16[64,66,1]{1,0,2:T(8,128)(2,1)S(1)} %collective-permute-done.3, bf16[64,66,1]{1,0,2:T(8,128)(2,1)S(1)} %collective-permute-done.2, bf16[64,1,512]{1,0,2:T(8,128)(2,1)} %copy.50, bf16[64,64,512]{1,0,2:T(8,128)(2,1)} %copy.49, bf16[64,1,512]{1,0,2:T(8,128)(2,1)} %copy.48), kind=kLoop, calls=%fused_computation.119 | loop fusion | flops 40301712 | bytes 8820240 | tf_op jit(solution)/shard_map/concatenate | solution.py:19
  214.8 119.0 %fusion.15 = f32[64,64,512]{1,0,2:T(8,128)} fusion(bf16[1,64,64,512]{2,1,3,0:T(8,128)(2,1)} %copy.61, bf16[1,64,64,512]{2,1,3,0:T(8,128)(2,1)} %copy.62, bf16[1,64,64,512]{2,1,3,0:T(8,128)(2,1)} %copy.63, bf16[64,64,512]{1,0,2:T(8,128)(2,1)} %copy.49, bf16[66,66,514]{1,0,2:T(8,128)(2,1)S(1)} %select_maximum_fusion, ...), kind=kLoop, calls=%fused_computation.26 | loop fusion | flops 293601280 | bytes 125960192 | tf_op jit(solution)/shard_map/add | solution.py:51
  333.9 12.7 %copy.56 = f32[64,64,512]{2,1,0:T(8,128)} copy(f32[64,64,512]{1,0,2:T(8,128)} %fusion.15) | data formatting | bytes 16777216 | tf_op jit(solution)/shard_map/add | solution.py:51
  346.6 1.6 broadcast_in_dim.32
  348.3 17.3 %multiply_reduce_fusion = (f32[]{:T(128)}, f32[4096,512]{1,0:T(8,128)}, bf16[4096,512]{1,0:T(8,128)(2,1)}, f32[4096,512]{1,0:T(8,128)S(1)}) fusion(bf16[64,64,512]{2,1,0:T(8,128)(2,1)} %param.5, f32[32,4096]{0,1:T(8,128)} %bitcast.295, f32[2,32,512]{2,1,0:T(8,128)S(1)} %copy-done.5, f32[4096,512]{1,0:T(8,128)} %fusion.124, f32[64,64,512]{2,1,0:T(8,128)} %copy.56), kind=kOutput, calls=%fused_computation.135 | convolution fusion | flops 822083584 | bytes 42532868 | tf_op jit(solution)/shard_map/dot_general | solution.py:67
  365.6 10.2 %convolution_bitcast_fusion.4 = f32[1,32,512]{2,1,0:T(8,128)S(1)} fusion(f32[4096,512]{1,0:T(8,128)} %get-tuple-element.16, f32[32,4096]{0,1:T(8,128)S(1)} %bitcast.294), kind=kOutput, calls=%fused_computation.142 | convolution fusion | flops 805306368 | bytes 8978432 | tf_op jit(solution)/shard_map/dot_general | solution.py:71
  375.8 7.7 %convolution_bitcast_fusion.1 = f32[32,4096]{1,0:T(8,128)S(1)} fusion(f32[4096,512]{1,0:T(8,128)S(1)} %copy-done, f32[2,32,512]{2,1,0:T(8,128)S(1)} %copy-done.5), kind=kOutput, calls=%fused_computation.137 | convolution fusion | flops 805306368 | bytes 8978432 | tf_op jit(solution)/shard_map/dot_general | solution.py:75
  383.5 0.0 copy-start.6
  383.6 5.3 convolution_bitcast_fusion.3
  388.8 8.0 %convolution_bitcast_fusion = f32[32,4096]{1,0:T(8,128)S(1)} fusion(f32[4096,512]{1,0:T(8,128)S(1)} %get-tuple-element.22, f32[2,32,512]{2,1,0:T(8,128)S(1)} %copy-done.5), kind=kOutput, calls=%fused_computation.136 | convolution fusion | flops 805306368 | bytes 8978432 | tf_op jit(solution)/shard_map/dot_general | solution.py:75
  396.8 68.7 %psum.52 = f32[]{:T(128)} all-reduce(f32[]{:T(128)} %get-tuple-element.15), channel_id=1, replica_groups=mesh['gy'=16,'gz'=8] {'gy','gz'}, use_global_device_ids=true, to_apply=%region_7.8 | all-reduce | flops 1 | bytes 8 | tf_op jit(solution)/shard_map/psum | solution.py:132
  465.5 0.6 copy.57
  466.1 2.0 copy.58
  468.1 2.2 maximum_reduce_fusion
  471.6 0.7 maximum_negate_fusion
  472.3 0.0 all-reduce.5.cloned.1.call-update
  472.3 26.1 %all-reduce.2 = (f32[32]{0:T(128)S(1)}, f32[1,32,8,8]{1,3,2,0:T(8,128)S(1)}, f32[2,32,8,8]{1,3,2,0:T(8,128)S(1)}) all-reduce(f32[32]{0:T(128)S(1)} %copy-done.8, f32[1,32,8,8]{1,3,2,0:T(8,128)S(1)} %bitcast.303, f32[2,32,8,8]{1,3,2,0:T(8,128)S(1)} %neg.13), channel_id=1, replica_groups=mesh['gy'=16,'gz'=8] {'gz'}, use_global_device_ids=true, to_apply=%region_5.6 | all-reduce | flops 6176 | bytes 49408 | tf_op jit(solution)/shard_map/psum | solution.py:133
  498.4 0.7 fusion.118
  499.1 105.1 %all-reduce.5.cloned.1.call-done = (f32[1,32,512]{2,1,0:T(8,128)}, f32[2,32,512]{2,1,0:T(8,128)}) async-done(((f32[1,32,512]{2,1,0:T(8,128)}, f32[2,32,512]{2,1,0:T(8,128)}), (f32[1,32,512]{2,1,0:T(8,128)}, f32[2,32,512]{2,1,0:T(8,128)})) %all-reduce.5.cloned.1.call-update) | async-done | bytes 196624 | tf_op jit(solution)/shard_map/psum | solution.py:140
  604.2 0.1 stack_broadcast_in_dim.5
  604.2 1.6 fusion.116
  (28 shorter events, 0.2 us)
Async XLA Ops:
  7.2 18.8 %copy-start.7 = (f32[2,32,8,8]{1,3,2,0:T(8,128)S(1)}, f32[2,32,8,8]{1,3,2,0:T(8,128)}, u32[]{:S(2)}) copy-start(f32[2,32,8,8]{1,3,2,0:T(8,128)} %param.8) | copy-start | bytes 49156
  7.2 18.8 %copy-start.5 = (f32[2,32,512]{2,1,0:T(8,128)S(1)}, f32[2,32,512]{2,1,0:T(8,128)}, u32[]{:S(2)}) copy-start(f32[2,32,512]{2,1,0:T(8,128)} %param.9) | copy-start | bytes 393220
  7.2 597.0 %all-reduce.5.cloned.1.call-start = ((), (), s32[]{:S(2)}) async-start(), calls=%async_computation | async-start | bytes 393216 | tf_op jit(solution)/shard_map/psum | solution.py:140
  8.7 54.8 %collective-permute-start = (bf16[64,1,512]{2,0,1:T(8,128)(2,1)S(1)}, bf16[64,1,512]{2,0,1:T(8,128)(2,1)S(1)}, u32[]{:S(2)}, u32[]{:S(2)}) collective-permute-start(bf16[64,1,512]{2,0,1:T(8,128)(2,1)S(1)} %copy.64), channel_id=1, source_target_pairs={{0,8},{8,16},{16,24},{24,32},{32,40},{40,48},{48,56},{56,64},{64,7... | collective-permute-start | bytes 196616 | tf_op jit(solution)/shard_map/ppermute | solution.py:21
  14.7 20.5 %copy-start.4 = (bf16[64,64,512]{2,1,0:T(8,128)(2,1)S(1)}, bf16[64,64,512]{2,1,0:T(8,128)(2,1)}, u32[]{:S(2)}) copy-start(bf16[64,64,512]{2,1,0:T(8,128)(2,1)} %param.5) | copy-start | bytes 12582916
  14.7 61.5 %collective-permute-start.1 = (bf16[64,1,512]{2,0,1:T(8,128)(2,1)S(1)}, bf16[64,1,512]{2,0,1:T(8,128)(2,1)S(1)}, u32[]{:S(2)}, u32[]{:S(2)}) collective-permute-start(bf16[64,1,512]{2,0,1:T(8,128)(2,1)S(1)} %copy.65), channel_id=1, source_target_pairs={{8,0},{16,8},{24,16},{32,24},{40,32},{48,40},{56,48},{64,56},{72,6... | collective-permute-start | bytes 196616 | tf_op jit(solution)/shard_map/ppermute | solution.py:23
  26.4 8.8 %copy-start.1 = (f32[32,64,8,8]{0,3,2,1:T(8,128)}, f32[32,64,8,8]{0,3,2,1:T(8,128)S(1)}, u32[]{:S(2)}) copy-start(f32[32,64,8,8]{0,3,2,1:T(8,128)S(1)} %broadcast_in_dim.28) | copy-start | bytes 1572868
  89.8 77.0 %collective-permute-start.2 = (bf16[64,66,1]{1,0,2:T(8,128)(2,1)S(1)}, bf16[64,66,1]{1,0,2:T(8,128)(2,1)S(1)}, u32[]{:S(2)}, u32[]{:S(2)}) collective-permute-start(bf16[64,66,1]{1,0,2:T(8,128)(2,1)S(1)} %get-tuple-element.10), channel_id=1, source_target_pairs={{0,1},{1,2},{2,3},{3,4},{4,5},{5,6},{6,7},{8,9},{9,10},{10,11},{11... | collective-permute-start | bytes 25352 | tf_op jit(solution)/shard_map/ppermute | solution.py:21
  93.0 73.8 %collective-permute-start.3 = (bf16[64,66,1]{1,0,2:T(8,128)(2,1)S(1)}, bf16[64,66,1]{1,0,2:T(8,128)(2,1)S(1)}, u32[]{:S(2)}, u32[]{:S(2)}) collective-permute-start(bf16[64,66,1]{1,0,2:T(8,128)(2,1)S(1)} %get-tuple-element.11), channel_id=1, source_target_pairs={{1,0},{2,1},{3,2},{4,3},{5,4},{6,5},{7,6},{9,8},{10,9},{11,10},{12... | collective-permute-start | bytes 25352 | tf_op jit(solution)/shard_map/ppermute | solution.py:23
  348.3 17.3 %copy-start.2 = (f32[32,64,8,8]{0,3,2,1:T(8,128)S(1)}, f32[32,64,8,8]{0,3,2,1:T(8,128)}, u32[]{:S(2)}) copy-start(f32[32,64,8,8]{0,3,2,1:T(8,128)} %copy-done.1) | copy-start | bytes 1572868
  365.6 10.2 %copy-start = (f32[4096,512]{1,0:T(8,128)S(1)}, f32[4096,512]{1,0:T(8,128)}, u32[]{:S(2)}) copy-start(f32[4096,512]{1,0:T(8,128)} %get-tuple-element.16) | copy-start | bytes 25165828
  365.6 18.0 %copy-start.3 = (f32[32,64,8,8]{0,3,2,1:T(8,128)S(1)}, f32[32,64,8,8]{0,3,2,1:T(8,128)}, u32[]{:S(2)}) copy-start(f32[32,64,8,8]{0,3,2,1:T(8,128)} %broadcast_in_dim.32) | copy-start | bytes 1572868
  383.5 88.8 %copy-start.6 = (f32[32,8,8]{0,2,1:T(8,128)S(1)}, f32[32,8,8]{0,2,1:T(8,128)}, u32[]{:S(2)}) copy-start(f32[32,8,8]{0,2,1:T(8,128)} %convolution_reduce_fusion) | copy-start | bytes 24580
  383.5 88.8 %copy-start.8 = (f32[32]{0:T(128)S(1)}, f32[32]{0:T(128)}, u32[]{:S(2)}) copy-start(f32[32]{0:T(128)} %broadcast_multiply_fusion) | copy-start | bytes 388
Sparse Core Ops, SparseCore 0:
  472.4 131.7 all-reduce.4
where the time goes:
time: 621 us; the launch traced here: 613 us
  other arithmetic  175 us (28%)
  blocking collectives  128 us (21%)
  local copies, waits for them, and re-layouts  106 us (17%)
  waiting for transfers between devices  105 us (17%)
  matrix products  70.4 us (11%)
  between operations  16.1 us (3%)
  starting transfers between devices  12.7 us (2%)
    add x1, other arithmetic, warp_image(): summed = summed + weight_x[along_x] * weight_y[along_y] * partial_z  119 us
    psum x1, waiting for transfers between devices, local(): lax.psum((grad_depth, first_depth, level_sum), 'gy')  105 us
    psum x1, blocking collectives, local(): energy = lax.psum(local_energy, ('gy', 'gz'))  68.7 us
    unnamed x24, local copies, waits for them, and re-layouts  52.3 us
    concatenate x2, other arithmetic, extended(): jnp.concatenate([lax.ppermute(tail, axis, [(i, (i + 1) % count) for i in...  48.1 us
    psum x1, blocking collectives, local(): lax.psum((grad_depth, first_depth, level_sum), 'gy')  32.9 us
    psum x1, blocking collectives, local(): lax.psum((grad_plane, first_diag, depth_level), 'gz')  26.1 us
    dot_general x2, matrix products, contract_rank(): lax.dot_general(left, right, (((0,), (0,)), ((), ())), precision=highest)  26.1 us
  transfers between devices with their start and end apart: 5, of which 1 were waited for; matrix products, arithmetic and copies ran while one was open for 16% of the time, Pallas kernels for 0%

commit v1 on v0

--- a/solution.py
+++ b/solution.py
@@ -129,7 +129,10 @@
     nodes_x = plane_factors.shape[2]
     nodes_y = plane_factors.shape[3] * lax.axis_size("gy")
     full_z = depth_factors.shape[2] * lax.axis_size("gz")
-    energy = lax.psum(local_energy, ("gy", "gz"))
+    tokens_scan = lambda mat, dev_axis, row_axis: jax.lax.psum(
+        jax.lax.psum(mat, axis_name=dev_axis), axis_name=row_axis
+    )
+    energy = tokens_scan(local_energy, "gy", "gz")
     grad_plane, first_diag, depth_level = lax.psum((grad_plane, first_diag, depth_level), "gz")
     diag_plane = jnp.stack(
         [first_diag, jnp.broadcast_to(depth_level[:, None, None], first_diag.shape)]

time: 621 us -> 591 us (0.952)
  blocking collectives: 128 us -> 62.6 us
  waiting for transfers between devices: 105 us -> 140 us
    psum x2 -> x1, blocking collectives: 102 us -> 33.5 us  [local(): jax.lax.psum(mat, axis_name=dev_axis)]
    psum x1, waiting for transfers between devices: 105 us -> 140 us  [local(): lax.psum((grad_depth, first_depth, level_sum), 'gy')]
  transfers between devices with their start and end apart: 5 -> 5, of which waited for: 1 -> 1; matrix products, arithmetic and copies ran while one was open for 16% -> 17% of each run, Pallas kernels for 0% -> 0%
where the time goes in v1:
time: 591 us; the launch traced here: 583 us
  other arithmetic  176 us (30%)
  waiting for transfers between devices  140 us (24%)
  local copies, waits for them, and re-layouts  106 us (18%)
  matrix products  70.8 us (12%)
  blocking collectives  62.6 us (11%)
  between operations  15.8 us (3%)
  starting transfers between devices  12.7 us (2%)
    psum x1, waiting for transfers between devices, local(): lax.psum((grad_depth, first_depth, level_sum), 'gy')  140 us
    add x1, other arithmetic, warp_image(): summed = summed + weight_x[along_x] * weight_y[along_y] * partial_z  119 us
    unnamed x24, local copies, waits for them, and re-layouts  52.1 us
    concatenate x2, other arithmetic, extended(): jnp.concatenate([lax.ppermute(tail, axis, [(i, (i + 1) % count) for i in...  48.3 us
    psum x1, blocking collectives, local(): jax.lax.psum(mat, axis_name=dev_axis)  33.5 us
    psum x1, blocking collectives, local(): lax.psum((grad_plane, first_diag, depth_level), 'gz')  29.1 us
    dot_general x2, matrix products, contract_rank(): lax.dot_general(left, right, (((0,), (0,)), ((), ())), precision=highest)  26.5 us
    dot_general x3, matrix products, contract_depth(): lax.dot_general(left, right, (((1,), (1,)), ((), ())), precision=highest)  23.1 us
  transfers between devices with their start and end apart: 5, of which 1 were waited for; matrix products, arithmetic and copies ran while one was open for 17% of the time, Pallas kernels for 0%

profile of v1, /device:TPU:7, one launch (start us, length us, event | category | flops | bytes accessed | tf_op | source)
XLA Modules:
  0.0 583.4 jit_solution(9409270871239238468)
XLA Ops:
  7.2 0.0 all-reduce.6.cloned.1.call-start
  7.2 1.4 fusion.133
  8.7 6.0 %collective-permute-start = (bf16[64,1,512]{2,0,1:T(8,128)(2,1)S(1)}, bf16[64,1,512]{2,0,1:T(8,128)(2,1)S(1)}, u32[]{:S(2)}, u32[]{:S(2)}) collective-permute-start(bf16[64,1,512]{2,0,1:T(8,128)(2,1)S(1)} %copy.64), channel_id=1, source_target_pairs={{0,8},{8,16},{16,24},{24,32},{32,40},{40,48},{48,56},{56,64},{64,7... | collective-permute-start | bytes 196616 | tf_op jit(solution)/shard_map/ppermute | solution.py:21
  14.7 0.0 copy-start.4
  14.7 2.2 collective-permute-start.1
  16.9 9.0 %fusion.132 = (bf16[1,64,64,512]{3,2,1,0:T(8,128)(2,1)}, bf16[1,64,64,512]{3,2,1,0:T(8,128)(2,1)}, bf16[1,64,64,512]{3,2,1,0:T(8,128)(2,1)}) fusion(bf16[3,64,64,512]{3,2,1,0:T(8,128)(2,1)} %param.7), kind=kLoop, calls=%fused_computation.173 | loop fusion | bytes 25165824 | tf_op jit(solution)/shard_map/slice | solution.py:39
  25.9 0.1 fusion.122
  26.1 0.3 broadcast_in_dim.28
  26.4 8.8 %fusion.124 = f32[4096,512]{1,0:T(8,128)} fusion(f32[32,4096]{0,1:T(8,128)S(1)} %bitcast.293, f32[2,32,512]{2,1,0:T(8,128)S(1)} %copy-done.5), kind=kOutput, calls=%fused_computation.159 | convolution fusion | flops 805306368 | bytes 10551296 | tf_op jit(solution)/shard_map/dot_general | solution.py:67
  35.2 1.2 convert_multiply_fusion
  36.4 7.5 %convolution_reduce_fusion = f32[32,8,8]{0,2,1:T(8,128)} fusion(f32[8,8,8,8,512]{4,3,2,1,0:T(8,128)S(1)} %bitcast.291, f32[2,32,512]{2,1,0:T(8,128)S(1)} %copy-done.5), kind=kOutput, calls=%fused_computation.139 | convolution fusion | flops 805451776 | bytes 8462336 | tf_op jit(solution)/shard_map/dot_general | solution.py:75
  43.9 0.3 broadcast_in_dim.34
  44.2 5.7 convolution_bitcast_fusion.2
  49.9 0.6 broadcast_multiply_fusion
  50.4 13.0 %copy.49 = bf16[64,64,512]{1,0,2:T(8,128)(2,1)} copy(bf16[64,64,512]{2,1,0:T(8,128)(2,1)} %param.6) | data formatting | bytes 8388608 | tf_op args[1]
  63.4 0.2 copy.59
  63.6 0.0 collective-permute-done
  63.6 12.7 %copy.48 = bf16[64,1,512]{1,0,2:T(8,128)(2,1)} copy(bf16[64,1,512]{2,0,1:T(8,128)(2,1)S(1)} %collective-permute-done) | data formatting | bytes 131072 | tf_op jit(solution)/shard_map/ppermute | solution.py:21
  76.2 12.7 %copy.50 = bf16[64,1,512]{1,0,2:T(8,128)(2,1)} copy(bf16[64,1,512]{2,0,1:T(8,128)(2,1)S(1)} %collective-permute-done.1) | data formatting | bytes 131072 | tf_op jit(solution)/shard_map/ppermute | solution.py:23
  88.9 0.9 pad_maximum_fusion.5
  89.8 3.2 collective-permute-start.2
  93.0 1.3 collective-permute-start.3
  94.3 0.3 broadcast_reduce_fusion
  94.7 13.2 %copy.61 = bf16[1,64,64,512]{2,1,3,0:T(8,128)(2,1)} copy(bf16[1,64,64,512]{3,2,1,0:T(8,128)(2,1)} %get-tuple-element.17) | data formatting | bytes 8388608
  107.8 13.0 %copy.62 = bf16[1,64,64,512]{2,1,3,0:T(8,128)(2,1)} copy(bf16[1,64,64,512]{3,2,1,0:T(8,128)(2,1)} %get-tuple-element.16) | data formatting | bytes 8388608
  120.8 12.9 %copy.63 = bf16[1,64,64,512]{2,1,3,0:T(8,128)(2,1)} copy(bf16[1,64,64,512]{3,2,1,0:T(8,128)(2,1)} %get-tuple-element.15) | data formatting | bytes 8388608
  133.7 24.1 %maximum_maximum_fusion = (bf16[64,66,513]{1,0,2:T(8,128)(2,1)S(1)}, bf16[64,66,513]{1,0,2:T(8,128)(2,1)}) fusion(bf16[64,1,512]{1,0,2:T(8,128)(2,1)} %copy.50, bf16[64,64,512]{1,0,2:T(8,128)(2,1)} %copy.49, bf16[64,1,512]{1,0,2:T(8,128)(2,1)} %copy.48, bf16[64,66,1]{1,0,2:T(8,128)(2,1)S(1)} %collective-permute-done.2, ...), kind=kLoop, calls=%fused_computation.126 | loop fusion | flops 34670592 | bytes 13009920 | tf_op jit(solution)/shard_map/concatenate | solution.py:19
  157.8 24.2 %select_maximum_fusion = bf16[66,66,514]{1,0,2:T(8,128)(2,1)S(1)} fusion(bf16[64,66,1]{1,0,2:T(8,128)(2,1)S(1)} %collective-permute-done.3, bf16[64,66,1]{1,0,2:T(8,128)(2,1)S(1)} %collective-permute-done.2, bf16[64,1,512]{1,0,2:T(8,128)(2,1)} %copy.50, bf16[64,64,512]{1,0,2:T(8,128)(2,1)} %copy.49, bf16[64,1,512]{1,0,2:T(8,128)(2,1)} %copy.48), kind=kLoop, calls=%fused_computation.119 | loop fusion | flops 40301712 | bytes 8820240 | tf_op jit(solution)/shard_map/concatenate | solution.py:19
  182.1 118.9 %fusion.15 = f32[64,64,512]{1,0,2:T(8,128)} fusion(bf16[1,64,64,512]{2,1,3,0:T(8,128)(2,1)} %copy.61, bf16[1,64,64,512]{2,1,3,0:T(8,128)(2,1)} %copy.62, bf16[1,64,64,512]{2,1,3,0:T(8,128)(2,1)} %copy.63, bf16[64,64,512]{1,0,2:T(8,128)(2,1)} %copy.49, bf16[66,66,514]{1,0,2:T(8,128)(2,1)S(1)} %select_maximum_fusion, ...), kind=kLoop, calls=%fused_computation.26 | loop fusion | flops 293601280 | bytes 125960192 | tf_op jit(solution)/shard_map/add | solution.py:51
  301.0 12.7 %copy.56 = f32[64,64,512]{2,1,0:T(8,128)} copy(f32[64,64,512]{1,0,2:T(8,128)} %fusion.15) | data formatting | bytes 16777216 | tf_op jit(solution)/shard_map/add | solution.py:51
  313.8 1.6 broadcast_in_dim.32
  315.4 17.8 %multiply_reduce_fusion = (f32[]{:T(128)}, f32[4096,512]{1,0:T(8,128)}, bf16[4096,512]{1,0:T(8,128)(2,1)}, f32[4096,512]{1,0:T(8,128)S(1)}) fusion(bf16[64,64,512]{2,1,0:T(8,128)(2,1)} %param.5, f32[32,4096]{0,1:T(8,128)} %bitcast.295, f32[2,32,512]{2,1,0:T(8,128)S(1)} %copy-done.5, f32[4096,512]{1,0:T(8,128)} %fusion.124, f32[64,64,512]{2,1,0:T(8,128)} %copy.56), kind=kOutput, calls=%fused_computation.135 | convolution fusion | flops 822083584 | bytes 42532868 | tf_op jit(solution)/shard_map/dot_general | solution.py:67
  333.2 10.2 %convolution_bitcast_fusion.4 = f32[1,32,512]{2,1,0:T(8,128)S(1)} fusion(f32[4096,512]{1,0:T(8,128)} %get-tuple-element.19, f32[32,4096]{0,1:T(8,128)S(1)} %bitcast.294), kind=kOutput, calls=%fused_computation.142 | convolution fusion | flops 805306368 | bytes 8978432 | tf_op jit(solution)/shard_map/dot_general | solution.py:71
  343.3 7.7 %convolution_bitcast_fusion.1 = f32[32,4096]{1,0:T(8,128)S(1)} fusion(f32[4096,512]{1,0:T(8,128)S(1)} %copy-done, f32[2,32,512]{2,1,0:T(8,128)S(1)} %copy-done.5), kind=kOutput, calls=%fused_computation.137 | convolution fusion | flops 805306368 | bytes 8978432 | tf_op jit(solution)/shard_map/dot_general | solution.py:75
  351.1 0.0 copy-start.6
  351.1 5.3 convolution_bitcast_fusion.3
  356.4 7.9 %convolution_bitcast_fusion = f32[32,4096]{1,0:T(8,128)S(1)} fusion(f32[4096,512]{1,0:T(8,128)S(1)} %get-tuple-element.25, f32[2,32,512]{2,1,0:T(8,128)S(1)} %copy-done.5), kind=kOutput, calls=%fused_computation.136 | convolution fusion | flops 805306368 | bytes 8978432 | tf_op jit(solution)/shard_map/dot_general | solution.py:75
  364.3 0.6 copy.57
  364.9 1.9 copy.58
  366.9 2.2 maximum_reduce_fusion
  369.1 33.5 %all-reduce.1 = (f32[]{:T(128)}, f32[32]{0:T(128)S(1)}) all-reduce(f32[]{:T(128)} %get-tuple-element.18, f32[32]{0:T(128)S(1)} %broadcast_reduce_fusion), channel_id=1, replica_groups=mesh['gy'=16,'gz'=8] {'gy'}, use_global_device_ids=true, to_apply=%region_7.8 | all-reduce | flops 33 | bytes 264 | tf_op jit(solution)/shard_map/psum | solution.py:133
  402.6 29.1 %all-reduce.3 = (f32[32]{0:T(128)S(1)}, f32[1,32,8,8]{1,3,2,0:T(8,128)S(1)}, f32[2,32,8,8]{1,3,2,0:T(8,128)S(1)}, f32[]{:T(128)}) all-reduce(f32[32]{0:T(128)S(1)} %copy-done.8, f32[1,32,8,8]{1,3,2,0:T(8,128)S(1)} %bitcast.303, f32[2,32,8,8]{1,3,2,0:T(8,128)S(1)} %neg.13, f32[]{:T(128)} %get-tuple-element.3), channel_id=1, replica_groups=mesh['gy'=16,'gz'=8] {'gz'}, use_global_device_ids=true, to_apply=%region_5.6 | all-reduce | flops 6177 | bytes 49416 | tf_op jit(solution)/shard_map/psum | solution.py:136
  433.1 0.7 maximum_negate_fusion
  433.7 0.0 all-reduce.6.cloned.1.call-update
  433.8 0.7 fusion.118
  434.4 140.2 %all-reduce.6.cloned.1.call-done = (f32[1,32,512]{2,1,0:T(8,128)}, f32[2,32,512]{2,1,0:T(8,128)}) async-done(((f32[1,32,512]{2,1,0:T(8,128)}, f32[2,32,512]{2,1,0:T(8,128)}), (f32[1,32,512]{2,1,0:T(8,128)}, f32[2,32,512]{2,1,0:T(8,128)})) %all-reduce.6.cloned.1.call-update) | async-done | bytes 196624 | tf_op jit(solution)/shard_map/psum | solution.py:143
  574.6 0.1 stack_broadcast_in_dim.5
  574.7 1.6 fusion.116
  (27 shorter events, 0.2 us)
Async XLA Ops:
  7.2 18.8 %copy-start.7 = (f32[2,32,8,8]{1,3,2,0:T(8,128)S(1)}, f32[2,32,8,8]{1,3,2,0:T(8,128)}, u32[]{:S(2)}) copy-start(f32[2,32,8,8]{1,3,2,0:T(8,128)} %param.8) | copy-start | bytes 49156
  7.2 18.8 %copy-start.5 = (f32[2,32,512]{2,1,0:T(8,128)S(1)}, f32[2,32,512]{2,1,0:T(8,128)}, u32[]{:S(2)}) copy-start(f32[2,32,512]{2,1,0:T(8,128)} %param.9) | copy-start | bytes 393220
  7.2 567.4 %all-reduce.6.cloned.1.call-start = ((), (), s32[]{:S(2)}) async-start(), calls=%async_computation | async-start | bytes 393216 | tf_op jit(solution)/shard_map/psum | solution.py:143
  8.7 54.9 %collective-permute-start = (bf16[64,1,512]{2,0,1:T(8,128)(2,1)S(1)}, bf16[64,1,512]{2,0,1:T(8,128)(2,1)S(1)}, u32[]{:S(2)}, u32[]{:S(2)}) collective-permute-start(bf16[64,1,512]{2,0,1:T(8,128)(2,1)S(1)} %copy.64), channel_id=1, source_target_pairs={{0,8},{8,16},{16,24},{24,32},{32,40},{40,48},{48,56},{56,64},{64,7... | collective-permute-start | bytes 196616 | tf_op jit(solution)/shard_map/ppermute | solution.py:21
  14.7 20.5 %copy-start.4 = (bf16[64,64,512]{2,1,0:T(8,128)(2,1)S(1)}, bf16[64,64,512]{2,1,0:T(8,128)(2,1)}, u32[]{:S(2)}) copy-start(bf16[64,64,512]{2,1,0:T(8,128)(2,1)} %param.5) | copy-start | bytes 12582916
  14.7 61.5 %collective-permute-start.1 = (bf16[64,1,512]{2,0,1:T(8,128)(2,1)S(1)}, bf16[64,1,512]{2,0,1:T(8,128)(2,1)S(1)}, u32[]{:S(2)}, u32[]{:S(2)}) collective-permute-start(bf16[64,1,512]{2,0,1:T(8,128)(2,1)S(1)} %copy.65), channel_id=1, source_target_pairs={{8,0},{16,8},{24,16},{32,24},{40,32},{48,40},{56,48},{64,56},{72,6... | collective-permute-start | bytes 196616 | tf_op jit(solution)/shard_map/ppermute | solution.py:23
  26.4 8.8 %copy-start.1 = (f32[32,64,8,8]{0,3,2,1:T(8,128)}, f32[32,64,8,8]{0,3,2,1:T(8,128)S(1)}, u32[]{:S(2)}) copy-start(f32[32,64,8,8]{0,3,2,1:T(8,128)S(1)} %broadcast_in_dim.28) | copy-start | bytes 1572868
  89.8 43.9 %collective-permute-start.2 = (bf16[64,66,1]{1,0,2:T(8,128)(2,1)S(1)}, bf16[64,66,1]{1,0,2:T(8,128)(2,1)S(1)}, u32[]{:S(2)}, u32[]{:S(2)}) collective-permute-start(bf16[64,66,1]{1,0,2:T(8,128)(2,1)S(1)} %get-tuple-element.13), channel_id=1, source_target_pairs={{0,1},{1,2},{2,3},{3,4},{4,5},{5,6},{6,7},{8,9},{9,10},{10,11},{11... | collective-permute-start | bytes 25352 | tf_op jit(solution)/shard_map/ppermute | solution.py:21
  93.0 40.7 %collective-permute-start.3 = (bf16[64,66,1]{1,0,2:T(8,128)(2,1)S(1)}, bf16[64,66,1]{1,0,2:T(8,128)(2,1)S(1)}, u32[]{:S(2)}, u32[]{:S(2)}) collective-permute-start(bf16[64,66,1]{1,0,2:T(8,128)(2,1)S(1)} %get-tuple-element.14), channel_id=1, source_target_pairs={{1,0},{2,1},{3,2},{4,3},{5,4},{6,5},{7,6},{9,8},{10,9},{11,10},{12... | collective-permute-start | bytes 25352 | tf_op jit(solution)/shard_map/ppermute | solution.py:23
  315.4 17.8 %copy-start.2 = (f32[32,64,8,8]{0,3,2,1:T(8,128)S(1)}, f32[32,64,8,8]{0,3,2,1:T(8,128)}, u32[]{:S(2)}) copy-start(f32[32,64,8,8]{0,3,2,1:T(8,128)} %copy-done.1) | copy-start | bytes 1572868
  333.2 10.2 %copy-start = (f32[4096,512]{1,0:T(8,128)S(1)}, f32[4096,512]{1,0:T(8,128)}, u32[]{:S(2)}) copy-start(f32[4096,512]{1,0:T(8,128)} %get-tuple-element.19) | copy-start | bytes 25165828
  333.2 17.9 %copy-start.3 = (f32[32,64,8,8]{0,3,2,1:T(8,128)S(1)}, f32[32,64,8,8]{0,3,2,1:T(8,128)}, u32[]{:S(2)}) copy-start(f32[32,64,8,8]{0,3,2,1:T(8,128)} %broadcast_in_dim.32) | copy-start | bytes 1572868
  351.1 51.6 %copy-start.6 = (f32[32,8,8]{0,2,1:T(8,128)S(1)}, f32[32,8,8]{0,2,1:T(8,128)}, u32[]{:S(2)}) copy-start(f32[32,8,8]{0,2,1:T(8,128)} %convolution_reduce_fusion) | copy-start | bytes 24580
  351.1 51.5 %copy-start.8 = (f32[32]{0:T(128)S(1)}, f32[32]{0:T(128)}, u32[]{:S(2)}) copy-start(f32[32]{0:T(128)} %broadcast_multiply_fusion) | copy-start | bytes 388
Sparse Core Ops, SparseCore 0:
  433.9 140.6 all-reduce.5
